TPU v7x, 512 devices: a whole 4x8x8 slice. The times are simulated.
512 devices in a mesh: cells: 128 (over y, z, core), samp: 4 (over x).
Axes of the slice: x: 4, y: 8, z: 8, core: 2. Of those that a mesh axis runs over, the one named last changes fastest.
Arguments:
- snapshots: bfloat16 [262144, 4096], P('cells', 'samp'), may hold values from -24 to 24
- left_slow: bfloat16 [120, 4096], P(None, 'cells'), may hold values from -0.09375 to 0.09375
- left_fast: bfloat16 [120, 64], replicated, may hold values from -0.75 to 0.75
- right_slow: bfloat16 [150, 128], P(None, 'samp'), may hold values from -0.5 to 0.5
- right_fast: bfloat16 [150, 32], replicated, may hold values from -1 to 1
Outputs:
- range_sketch: float32 [262144, 150], P(('cells', 'samp'))
- core: float32 [150, 4096], P(None, ('samp', 'cells'))
All inputs are finite; a program needn't handle non-finite values.
Results may differ from a plain program's by a relative error of at most 0.012.
The roundings to bfloat16 on the way count: a program that leaves them out, or rounds other values in their place, can miss the bound.
Values sent between devices are 32-bit elements; how exact they have to be, the bound alone decides.
A program may use at most 64 MiB of HBM per device.

v0:
```python
import jax
import jax.numpy as jnp
from jax import lax
from jax.sharding import PartitionSpec as P


def expand(slow, fast):
    rows = slow.shape[0]
    return (
        (slow.astype(jnp.float32)[:, :, None] * fast.astype(jnp.float32)[:, None, :])
        .reshape(rows, -1)
        .astype(jnp.bfloat16)
    )


def on_device(snapshots, left_slow, left_fast, right_slow, right_fast):
    psi = expand(left_slow, left_fast)
    omega = expand(right_slow, right_fast)
    left_term = jnp.dot(psi, snapshots, preferred_element_type=jnp.float32)
    range_term = lax.dot_general(
        snapshots, omega, (((1,), (1,)), ((), ())), preferred_element_type=jnp.float32
    )
    range_part = lax.psum_scatter(range_term, "samp", scatter_dimension=0, tiled=True)
    width = snapshots.shape[1] // lax.axis_size("cells")
    col_start = lax.axis_index("cells") * width
    left_full = lax.psum(left_term, "cells")
    left_part = lax.dynamic_slice_in_dim(left_full, col_start, width, 1)
    height = range_part.shape[0]
    psi_rows = lax.dynamic_slice_in_dim(psi, lax.axis_index("samp") * height, height, 1).astype(
        jnp.float32
    )
    partial_value = jnp.dot(psi_rows, range_part, precision=lax.Precision.HIGHEST)
    core_input = lax.psum(partial_value, ("cells", "samp"))
    rank_left = core_input.shape[0]
    gram = jnp.dot(core_input, core_input.T, precision=lax.Precision.HIGHEST) + 0.5 * jnp.eye(
        rank_left, dtype=jnp.float32
    )
    factor = jnp.linalg.cholesky(gram)
    solved = jax.scipy.linalg.cho_solve((factor, True), left_part)
    core = jnp.dot(core_input.T, solved, precision=lax.Precision.HIGHEST)
    return (range_part, core)


def solution(mesh):
    placed = (P("cells", "samp"), P(None, "cells"), P(), P(None, "samp"), P())
    return jax.shard_map(
        on_device,
        mesh=mesh,
        in_specs=placed,
        out_specs=(P(("cells", "samp"), None), P(None, ("samp", "cells"))),
        check_vma=False,
    )
```

profile of v0, /device:TPU:24, one launch (start us, length us, event | category | flops | bytes accessed | tf_op | source)
XLA Modules:
  0.0 517.7 jit_solution(6661757169224194869)
XLA Ops:
  7.2 0.0 copy-start
  7.2 0.0 copy-start.1
  7.2 0.0 reduce-scatter.2.cloned.1.call-start
  7.2 0.7 convert_element_type.27
  8.0 0.7 convert_element_type.26
  8.7 0.1 multiply_convert_fusion.1
  8.8 4.8 convolution_bitcast_fusion
  13.6 0.0 reduce-scatter.2.cloned.1.call-update
  13.6 0.0 all-reduce.3.cloned.1.call-start
  13.7 0.0 copy-done
  13.7 0.0 copy-done.1
  13.7 0.1 multiply_convert_fusion
  13.9 34.2 %reduce-scatter.2.cloned.1.call-done = f32[512,150]{0,1:T(8,128)} async-done(((f32[2048,150]{0,1:T(8,128)}), f32[512,150]{0,1:T(8,128)}) %reduce-scatter.2.cloned.1.call-update) | async-done | bytes 307216 | tf_op jit(solution)/shard_map/reduce_scatter | solution.py:23
  48.0 1.9 fusion
  49.9 0.0 all-reduce.3.cloned.1.call-update
  49.9 0.0 all-reduce.5.cloned.1.call-start
  50.0 3.7 fusion.13
  53.7 0.0 all-reduce.5.cloned.1.call-update
  53.7 261.5 %all-reduce.3.cloned.1.call-done = f32[120,150]{0,1:T(8,128)} async-done(((f32[120,150]{0,1:T(8,128)}), f32[120,150]{0,1:T(8,128)}) %all-reduce.3.cloned.1.call-update) | async-done | bytes 72016 | tf_op jit(solution)/shard_map/psum | solution.py:33
  315.2 1.4 fusion.12
  316.6 0.1 copy.12
  316.7 11.0 %cholesky.16 = f32[120,120]{1,0:T(8,128)S(1)} custom-call(f32[120,120]{1,0:T(8,128)S(1)} %fusion.8), custom_call_target="Cholesky" | custom-call | tf_op jit(solution)/shard_map/jit(cholesky)/cholesky | solution.py:38
  327.8 0.6 compare_reduce_fusion
  328.4 0.7 fusion.2
  329.1 9.2 %custom-call.10 = f32[1,120,120]{1,2,0:T(8,128)S(1)} custom-call(f32[1,120,120]{2,1,0:T(8,128)S(1)} %fusion.2), custom_call_target="InvertDiagBlocksLowerTriangular" | custom-call | tf_op jit(solution)/shard_map/jit(_cho_solve)/triangular_solve | solution.py:39
  338.3 169.8 %all-reduce.5.cloned.1.call-done = f32[120,1024]{1,0:T(8,128)} async-done(((f32[120,1024]{1,0:T(8,128)}), f32[120,1024]{1,0:T(8,128)}) %all-reduce.5.cloned.1.call-update) | async-done | bytes 491536 | tf_op jit(solution)/shard_map/psum | solution.py:26
  508.0 1.2 fusion.5
  509.2 0.2 fusion.3
  509.5 1.8 fusion.14
  (4 shorter events, 0.1 us)
Async XLA Ops:
  7.2 6.5 %copy-start = (bf16[120,64]{0,1:T(8,128)(2,1)S(1)}, bf16[120,64]{0,1:T(8,128)(2,1)}, u32[]{:S(2)}) copy-start(bf16[120,64]{0,1:T(8,128)(2,1)} %param.7) | copy-start | bytes 46084
  7.2 6.5 %copy-start.1 = (bf16[120,32]{0,1:T(8,128)(2,1)S(1)}, bf16[120,32]{0,1:T(8,128)(2,1)}, u32[]{:S(2)}) copy-start(bf16[120,32]{0,1:T(8,128)(2,1)} %param.6) | copy-start | bytes 23044
  7.2 40.8 %reduce-scatter.2.cloned.1.call-start = ((), (), s32[]{:S(2)}) async-start(), calls=%async_computation.1 | async-start | bytes 1556480 | tf_op jit(solution)/shard_map/reduce_scatter | solution.py:23
  13.6 301.6 %all-reduce.3.cloned.1.call-start = ((), (), s32[]{:S(2)}) async-start(), calls=%async_computation.2 | async-start | bytes 155648 | tf_op jit(solution)/shard_map/psum | solution.py:33
  49.9 458.1 %all-reduce.5.cloned.1.call-start = ((), (), s32[]{:S(2)}) async-start(), calls=%async_computation.3 | async-start | bytes 983040 | tf_op jit(solution)/shard_map/psum | solution.py:26
Sparse Core Ops, SparseCore 0:
  13.7 34.2 reduce-scatter.1
  53.0 262.1 all-reduce.2
  318.5 189.4 all-reduce.4
where the time goes:
time: 518 us
  waiting for transfers between devices  465 us (90%)
  other arithmetic  23.2 us (4%)
  matrix products  15 us (3%)
  between operations  13.9 us (3%)
    psum x1, waiting for transfers between devices, on_device(): core_input = lax.psum(partial_value, ('cells', 'samp'))  261 us
    psum x1, waiting for transfers between devices, on_device(): left_full = lax.psum(left_term, 'cells')  170 us
    reduce_scatter x1, waiting for transfers between devices, on_device(): lax.psum_scatter(range_term, 'samp', scatter_dimension=0, tiled=True)  34.2 us
    another operation x3, other arithmetic, on_device(): factor = jnp.linalg.cholesky(gram)  11.6 us
  transfers between devices with their start and end apart: 3, of which 3 were waited for; matrix products, arithmetic and copies ran while one was open for 5% of the time, Pallas kernels for 0%

commit v1 on v0

--- a/solution.py
+++ b/solution.py
@@ -30,7 +30,7 @@
         jnp.float32
     )
     partial_value = jnp.dot(psi_rows, range_part, precision=lax.Precision.HIGHEST)
-    core_input = lax.psum(partial_value, ("cells", "samp"))
+    core_input = lax.psum(lax.psum(partial_value, "samp"), "cells")
     rank_left = core_input.shape[0]
     gram = jnp.dot(core_input, core_input.T, precision=lax.Precision.HIGHEST) + 0.5 * jnp.eye(
         rank_left, dtype=jnp.float32

time: 518 us -> 335 us (0.65)
  the two profiles are of different devices: /device:TPU:24 before, /device:TPU:1 now
where the time goes in v1:
time: 335 us
  waiting for transfers between devices  282 us (84%)
  other arithmetic  23.2 us (7%)
  matrix products  14.9 us (4%)
  between operations  13.9 us (4%)
    psum x2, waiting for transfers between devices, on_device(): core_input = lax.psum(lax.psum(partial_value, 'samp'), 'cells')  249 us
    reduce_scatter x1, waiting for transfers between devices, on_device(): lax.psum_scatter(range_term, 'samp', scatter_dimension=0, tiled=True)  33.1 us
    another operation x3, other arithmetic, on_device(): factor = jnp.linalg.cholesky(gram)  11.6 us
    another operation x2, other arithmetic, on_device(): solved = jax.scipy.linalg.cho_solve((factor, True), left_part)  9.85 us
  transfers between devices with their start and end apart: 3, of which 3 were waited for; matrix products, arithmetic and copies ran while one was open for 1% of the time, Pallas kernels for 0%

profile of v1, /device:TPU:1, one launch (start us, length us, event | category | flops | bytes accessed | tf_op | source)
XLA Modules:
  0.0 334.7 jit_solution(13868642109355701146)
XLA Ops:
  7.2 0.0 copy-start
  7.2 0.0 copy-start.1
  7.2 0.0 reduce-scatter.2.cloned.1.call-start
  7.2 0.7 convert_element_type.27
  8.0 0.7 convert_element_type.26
  8.7 0.1 multiply_convert_fusion.1
  8.8 4.8 %convolution_bitcast_fusion = f32[2048,150]{0,1:T(8,128)} fusion(bf16[150,1024]{0,1:T(8,128)(2,1)S(1)} %bitcast.29, bf16[2048,1024]{1,0:T(8,128)(2,1)} %param.5), kind=kOutput, calls=%fused_computation | convolution fusion | flops 629145600 | bytes 5730304 | tf_op jit(solution)/shard_map/dot_general | solution.py:20
  13.6 0.0 reduce-scatter.2.cloned.1.call-update
  13.6 0.0 all-reduce.4.cloned.1.call-start
  13.7 0.0 copy-done
  13.7 0.0 copy-done.1
  13.7 0.1 multiply_convert_fusion
  13.9 33.1 %reduce-scatter.2.cloned.1.call-done = f32[512,150]{0,1:T(8,128)} async-done(((f32[2048,150]{0,1:T(8,128)}), f32[512,150]{0,1:T(8,128)}) %reduce-scatter.2.cloned.1.call-update) | async-done | bytes 307216 | tf_op jit(solution)/shard_map/reduce_scatter | solution.py:23
  46.9 1.9 fusion
  48.8 0.0 all-reduce.4.cloned.1.call-update
  48.8 0.0 all-reduce.6.cloned.1.call-start
  48.9 3.7 %fusion.13 = f32[120,1024]{1,0:T(8,128)} fusion(bf16[120,2048]{0,1:T(8,128)(2,1)S(1)} %bitcast.28, bf16[2048,1024]{1,0:T(8,128)(2,1)} %param.5), kind=kOutput, calls=%fused_computation.23 | convolution fusion | flops 503316480 | bytes 5177344 | tf_op jit(solution)/shard_map/dot_general | solution.py:19
  52.6 47.6 %all-reduce.4.cloned.1.call-done = f32[120,150]{0,1:T(8,128)} async-done(((f32[120,150]{0,1:T(8,128)}), f32[120,150]{0,1:T(8,128)}) %all-reduce.4.cloned.1.call-update) | async-done | bytes 72016 | tf_op jit(solution)/shard_map/psum | solution.py:33
  100.2 0.0 all-reduce.6.cloned.1.call-update
  100.2 201.8 %all-reduce.6.cloned.1.call-done = (f32[120,150]{0,1:T(8,128)}, f32[120,1024]{1,0:T(8,128)}) async-done(((f32[120,150]{0,1:T(8,128)}, f32[120,1024]{1,0:T(8,128)}), (f32[120,150]{0,1:T(8,128)}, f32[120,1024]{1,0:T(8,128)})) %all-reduce.6.cloned.1.call-update) | async-done | bytes 563536 | tf_op jit(solution)/shard_map/psum | solution.py:33
  301.9 1.4 fusion.12
  303.3 0.1 copy.12
  303.5 11.0 %cholesky.16 = f32[120,120]{1,0:T(8,128)S(1)} custom-call(f32[120,120]{1,0:T(8,128)S(1)} %fusion.8), custom_call_target="Cholesky" | custom-call | tf_op jit(solution)/shard_map/jit(cholesky)/cholesky | solution.py:38
  314.5 0.6 compare_reduce_fusion
  315.1 0.7 fusion.2
  315.8 9.2 %custom-call.10 = f32[1,120,120]{1,2,0:T(8,128)S(1)} custom-call(f32[1,120,120]{2,1,0:T(8,128)S(1)} %fusion.2), custom_call_target="InvertDiagBlocksLowerTriangular" | custom-call | tf_op jit(solution)/shard_map/jit(_cho_solve)/triangular_solve | solution.py:39
  325.0 1.2 fusion.5
  326.2 0.3 fusion.3
  326.4 1.8 fusion.14
  (4 shorter events, 0.1 us)
Async XLA Ops:
  7.2 6.5 %copy-start = (bf16[120,64]{0,1:T(8,128)(2,1)S(1)}, bf16[120,64]{0,1:T(8,128)(2,1)}, u32[]{:S(2)}) copy-start(bf16[120,64]{0,1:T(8,128)(2,1)} %param.7) | copy-start | bytes 46084
  7.2 6.5 %copy-start.1 = (bf16[120,32]{0,1:T(8,128)(2,1)S(1)}, bf16[120,32]{0,1:T(8,128)(2,1)}, u32[]{:S(2)}) copy-start(bf16[120,32]{0,1:T(8,128)(2,1)} %param.6) | copy-start | bytes 23044
  7.2 39.8 %reduce-scatter.2.cloned.1.call-start = ((), (), s32[]{:S(2)}) async-start(), calls=%async_computation.1 | async-start | bytes 1556480 | tf_op jit(solution)/shard_map/reduce_scatter | solution.py:23
  13.6 86.5 %all-reduce.4.cloned.1.call-start = ((), (), s32[]{:S(2)}) async-start(), calls=%async_computation.2 | async-start | bytes 155648 | tf_op jit(solution)/shard_map/psum | solution.py:33
  48.8 253.1 %all-reduce.6.cloned.1.call-start = ((), (), s32[]{:S(2)}) async-start(), calls=%async_computation.3 | async-start | bytes 1138688 | tf_op jit(solution)/shard_map/psum | solution.py:33
Sparse Core Ops, SparseCore 0:
  13.7 33.1 reduce-scatter.1
  49.3 50.8 all-reduce.3
  103.6 198.3 all-reduce.5
